TPU v7x, 128 devices: a whole 4x4x4 slice. The times are simulated.
128 devices in a mesh: kz: 8 (over x_hi, z), en: 16 (over y, x_lo, core).
Axes of the slice: x: 4 (x_hi: 2, x_lo: 2; x = x_hi * 2 + x_lo), y: 4, z: 4, core: 2. Of those that a mesh axis runs over, the one named last changes fastest.
Arguments:
- green_lesser: bfloat16 [8, 32, 2, 512, 512], P('kz', 'en'), may hold values from -6 to 6
- coupling: float32 [3, 4, 2, 128, 128], replicated, may hold values from -0.25 to 0.25
- block_list: int32 [3, 4, 2], replicated, may hold values from 0 to 3, as said below
- offsets: int32 [3], replicated, may hold values from -1 to 1, as said below
- shifts: int32 [3], replicated, may hold values from 1 to 2, as said below
- occupation: float32 [3], replicated, may hold values from 0.25 to 4
Outputs:
- sigma_lesser: float32 [8, 32, 2, 512, 512], P('kz', 'en')
Inputs may be any that keep to these rules, and one draw needn't show every extreme that they name: `block_list`: for each transfer, the 4 listed blocks hold every block row once and every block column once. -1 and +1 each occur among the offsets. 1 and 2 each occur among the shifts.
All inputs are finite; a program needn't handle non-finite values.
Results may differ from a plain program's by a relative error of at most 0.0057.
Values may be sent and summed in bfloat16 or wider, within the bound.
A program may use at most 128 MiB of HBM per device.

v0:
```python
import jax
import jax.numpy as jnp
from jax import lax
from jax.sharding import PartitionSpec as P

NQ = 3
SMAX = 2


def padded(block, sides, width, periodic):
    for axis, dim in sides:
        count = lax.axis_size(axis)
        forward = [(i, i + 1) for i in range(count - 1)]
        if periodic:
            forward.append((count - 1, 0))
        backward = [(target, source) for source, target in forward]
        low = lax.ppermute(
            lax.slice_in_dim(block, block.shape[dim] - width, None, axis=dim), axis, forward
        )
        high = lax.ppermute(lax.slice_in_dim(block, 0, width, axis=dim), axis, backward)
        block = jnp.concatenate([low, block, high], axis=dim)
    return block


def sandwich(field, blocks, row_index, column_index):
    batch_count = field.shape[0]
    orbitals = field.shape[-1]
    block_size = blocks.shape[-1]
    block_count = orbitals // block_size
    real_part = blocks[:, 0]
    imag_part = blocks[:, 1]
    numbers = jnp.arange(block_count, dtype=jnp.int32)
    matches = (row_index[:, None] == numbers[None, :]).astype(jnp.int32)
    inverse = jnp.sum(numbers[:, None] * matches, axis=0)
    row_blocks = field.reshape(batch_count, 2, block_count, block_size, orbitals)
    picked = jnp.take(row_blocks, column_index, axis=2)

    def product_left(matrix, other):
        return jnp.einsum("nxy,lnyo->lnxo", matrix, other, preferred_element_type=jnp.float32)

    left_real = product_left(real_part, picked[:, 0]) - product_left(imag_part, picked[:, 1])
    left_imag = product_left(real_part, picked[:, 1]) + product_left(imag_part, picked[:, 0])
    products = jnp.stack([left_real.astype(jnp.bfloat16), left_imag.astype(jnp.bfloat16)], axis=1)
    left_half = jnp.take(products, inverse, axis=2)
    column_blocks = left_half.reshape(batch_count, 2, orbitals, block_count, block_size)
    chosen = jnp.take(column_blocks, column_index, axis=3)

    def product_right(other, matrix):
        return jnp.einsum("lony,nxy->lonx", other, matrix, preferred_element_type=jnp.float32)

    right_real = product_right(chosen[:, 0], real_part) + product_right(chosen[:, 1], imag_part)
    right_imag = product_right(chosen[:, 1], real_part) - product_right(chosen[:, 0], imag_part)
    stacked = jnp.stack([right_real, right_imag], axis=1)
    result = jnp.take(stacked, inverse, axis=3)
    return result.reshape(batch_count, 2, orbitals, orbitals)


def on_device(green_lesser, coupling, block_list, offsets, shifts, occupation):
    coupling_rounded = coupling.astype(jnp.bfloat16)
    momenta_here = green_lesser.shape[0]
    energies_here = green_lesser.shape[1]
    orbitals = green_lesser.shape[-1]
    widened = padded(green_lesser, (("kz", 0),), 1, True)
    widened = padded(widened, (("en", 1),), SMAX, False)
    sigma_sum = jnp.zeros(green_lesser.shape, jnp.float32)
    for transfer in range(NQ):
        start_momentum = 1 - offsets[transfer]
        source_rows = lax.dynamic_slice_in_dim(widened, start_momentum, momenta_here, 0)
        absorbed = lax.dynamic_slice_in_dim(source_rows, SMAX - shifts[transfer], energies_here, 1)
        emitted = lax.dynamic_slice_in_dim(source_rows, SMAX + shifts[transfer], energies_here, 1)
        weight = occupation[transfer]
        combined = (
            weight * absorbed.astype(jnp.float32) + (weight + 1.0) * emitted.astype(jnp.float32)
        ).astype(jnp.bfloat16)
        flattened = combined.reshape(momenta_here * energies_here, 2, orbitals, orbitals)
        term = sandwich(
            flattened,
            coupling_rounded[transfer],
            block_list[transfer, :, 0],
            block_list[transfer, :, 1],
        )
        sigma_sum = sigma_sum + term.reshape(green_lesser.shape)
    return sigma_sum


def solution(mesh):
    placed = (P("kz", "en", None, None, None), P(), P(), P(), P(), P())
    return jax.shard_map(
        on_device,
        mesh=mesh,
        in_specs=placed,
        out_specs=P("kz", "en", None, None, None),
        check_vma=False,
    )
```

profile of v0, /device:TPU:1, one launch (start us, length us, event | category | flops | bytes accessed | tf_op | source)
XLA Modules:
  0.0 365.7 jit_solution(6746407249563565672)
XLA Ops:
  0.0 2.5 collective-permute-start
  2.5 4.6 %collective-permute-start.1 = (bf16[1,2,2,512,512]{4,3,2,1,0:T(8,128)(2,1)}, bf16[1,2,2,512,512]{4,3,2,1,0:T(8,128)(2,1)S(1)}, u32[]{:S(2)}, u32[]{:S(2)}) collective-permute-start(bf16[1,2,2,512,512]{4,3,2,1,0:T(8,128)(2,1)} %param.12), channel_id=1, source_target_pairs={{16,0},{32,16},{48,32},{64,48},{80,64},{96,80},{112,96},{0,112},{1... | collective-permute-start | bytes 6291464 | tf_op jit(solution)/shard_map/ppermute | solution.py:20
  7.1 45.5 %collective-permute-done = bf16[1,2,2,512,512]{4,3,2,1,0:T(8,128)(2,1)S(1)} collective-permute-done((bf16[1,2,2,512,512]{4,3,2,1,0:T(8,128)(2,1)}, bf16[1,2,2,512,512]{4,3,2,1,0:T(8,128)(2,1)S(1)}, u32[]{:S(2)}, u32[]{:S(2)}) %collective-permute-start) | collective-permute-done | bytes 2097184 | tf_op jit(solution)/shard_map/ppermute | solution.py:17
  57.1 3.1 collective-permute-start.3
  60.2 2.4 collective-permute-start.2
  78.0 115.6 %collective-permute-done.3 = bf16[3,2,2,512,512]{4,3,2,1,0:T(8,128)(2,1)} collective-permute-done((bf16[3,2,2,512,512]{4,3,2,1,0:T(8,128)(2,1)}, bf16[3,2,2,512,512]{4,3,2,1,0:T(8,128)(2,1)}, u32[]{:S(2)}, u32[]{:S(2)}) %collective-permute-start.3) | collective-permute-done | bytes 6291488 | tf_op jit(solution)/shard_map/ppermute | solution.py:20
  193.6 9.6 %pad_maximum_fusion = bf16[3,6,2,512,512]{4,3,2,1,0:T(8,128)(2,1)S(1)} fusion(bf16[3,2,2,512,512]{4,3,2,1,0:T(8,128)(2,1)} %collective-permute-done.3, bf16[3,2,2,512,512]{4,3,2,1,0:T(8,128)(2,1)} %constant_dynamic-update-slice_fusion, bf16[3,2,2,512,512]{4,3,2,1,0:T(8,128)(2,1)} %collective-permute-done.2), kind=kLoop, calls=%fused_computation.12 | loop fusion | flops 18874368 | bytes 37748736 | tf_op jit(solution)/shard_map/concatenate | solution.py:21
  203.2 5.8 %add_convert_fusion.2 = (bf16[1,2,2,512,512]{4,3,2,1,0:T(8,128)(2,1)}, bf16[1,2,2,512,512]{4,3,2,1,0:T(8,128)(2,1)S(1)}, bf16[1,2,2,512,512]{4,3,2,1,0:T(8,128)(2,1)}) fusion(bf16[3,6,2,512,512]{4,3,2,1,0:T(8,128)(2,1)S(1)} %pad_maximum_fusion, s32[]{:T(128)S(6)} %select_n.65, s32[]{:T(128)S(6)} %select_n.69, f32[]{:T(128)S(6)} %add.195, s32[]{:T(128)S(6)} %select_n.67, ...), kind=kLoop, calls=%fused_computation.20 | loop fusion | flops 18874368 | bytes 18874428 | tf_op jit(solution)/shard_map/convert_element_type | solution.py:74
  211.0 3.0 copy.32
  222.6 4.0 %reshape.99 = bf16[2,2,512,4,128]{4,3,2,1,0:T(4,128)(2,1)} reshape(bf16[2,2,4,128,512]{4,3,2,1,0:T(8,128)(2,1)} %copy.33) | data formatting | bytes 4194304 | tf_op jit(solution)/shard_map/reshape | solution.py:45
  236.1 3.6 gather_fusion.4
  239.8 4.1 %copy.28 = bf16[4,2,2,128,512]{3,4,1,0,2:T(8,128)(2,1)} copy(bf16[4,2,2,128,512]{4,3,2,1,0:T(8,128)(2,1)} %gather_fusion.4) | data formatting | bytes 4194304 | tf_op jit(solution)/shard_map/jit(_take)/gather | solution.py:36
  249.1 3.8 %gather_fusion.5 = bf16[4,2,2,128,512]{3,4,1,2,0:T(8,128)(2,1)} fusion(bf16[2,2,4,128,512]{3,4,0,2,1:T(8,128)(2,1)} %pad_maximum_fusion.5, s32[1024]{0:T(1024)S(1)} %pad_clamp_fusion.2), kind=kCustom, calls=%fused_computation.5.clone | custom fusion | bytes 4194320 | tf_op jit(solution)/shard_map/jit(_take)/gather | solution.py:44
  252.9 3.2 select_bitcast_fusion.2
  256.1 4.1 %copy.29 = bf16[2,2,4,128,512]{4,3,2,1,0:T(8,128)(2,1)} copy(bf16[2,2,4,128,512]{3,4,0,1,2:T(8,128)(2,1)} %select_bitcast_fusion.2) | data formatting | bytes 4194304 | tf_op jit(solution)/shard_map/jit(_take)/select_n | solution.py:44
  260.2 4.0 %reshape.98 = bf16[2,2,512,4,128]{4,3,2,1,0:T(4,128)(2,1)} reshape(bf16[2,2,4,128,512]{4,3,2,1,0:T(8,128)(2,1)} %copy.29) | data formatting | bytes 4194304 | tf_op jit(solution)/shard_map/reshape | solution.py:45
  264.2 3.4 copy.30
  267.6 3.8 %gather_fusion.6 = bf16[4,2,2,512,128]{4,3,2,1,0:T(8,128)(2,1)} fusion(bf16[2,2,512,4,128]{4,2,3,1,0:T(8,128)(2,1)} %copy.30, s32[1024]{0:T(1024)S(1)} %pad_clamp_fusion.3), kind=kCustom, calls=%fused_computation.8.clone | custom fusion | bytes 4194320 | tf_op jit(solution)/shard_map/jit(_take)/gather | solution.py:46
  277.1 3.6 gather_fusion
  280.7 4.1 %copy.23 = bf16[4,2,2,128,512]{3,4,1,0,2:T(8,128)(2,1)} copy(bf16[4,2,2,128,512]{4,3,2,1,0:T(8,128)(2,1)} %gather_fusion) | data formatting | bytes 4194304 | tf_op jit(solution)/shard_map/jit(_take)/gather | solution.py:36
  289.9 3.7 %gather_fusion.1 = bf16[4,2,2,128,512]{3,4,1,2,0:T(8,128)(2,1)} fusion(bf16[2,2,4,128,512]{3,4,0,2,1:T(8,128)(2,1)} %pad_maximum_fusion.4, s32[1024]{0:T(1024)S(1)} %pad_clamp_fusion.4), kind=kCustom, calls=%fused_computation.3.clone | custom fusion | bytes 4194320 | tf_op jit(solution)/shard_map/jit(_take)/gather | solution.py:44
  293.6 3.2 select_bitcast_fusion.4
  296.8 4.1 %copy.25 = bf16[2,2,4,128,512]{4,3,2,1,0:T(8,128)(2,1)} copy(bf16[2,2,4,128,512]{3,4,0,1,2:T(8,128)(2,1)} %select_bitcast_fusion.4) | data formatting | bytes 4194304 | tf_op jit(solution)/shard_map/jit(_take)/select_n | solution.py:44
  300.9 4.0 %reshape.97 = bf16[2,2,512,4,128]{4,3,2,1,0:T(4,128)(2,1)} reshape(bf16[2,2,4,128,512]{4,3,2,1,0:T(8,128)(2,1)} %copy.25) | data formatting | bytes 4194304 | tf_op jit(solution)/shard_map/reshape | solution.py:45
  304.9 3.3 copy.26
  308.2 3.7 %gather_fusion.2 = bf16[4,2,2,512,128]{4,3,2,1,0:T(8,128)(2,1)} fusion(bf16[2,2,512,4,128]{4,2,3,1,0:T(8,128)(2,1)} %copy.26, s32[1024]{0:T(1024)S(1)} %pad_clamp_fusion.5), kind=kCustom, calls=%fused_computation.1.clone | custom fusion | bytes 4194320 | tf_op jit(solution)/shard_map/jit(_take)/gather | solution.py:46
  322.2 5.1 %gather_fusion.11 = f32[4,2,2,512,128]{4,3,1,2,0:T(8,128)} fusion(f32[2,2,512,4,128]{4,2,0,3,1:T(8,128)} %pad_maximum_fusion.3, s32[1024]{0:T(1024)S(1)} %pad_clamp_fusion), kind=kCustom, calls=%fused_computation.11.clone | custom fusion | bytes 8388624 | tf_op jit(solution)/shard_map/jit(_take)/gather | solution.py:54
  332.3 5.1 %gather_fusion.7 = f32[4,2,2,512,128]{4,3,1,2,0:T(8,128)} fusion(f32[2,2,512,4,128]{4,2,0,3,1:T(8,128)} %pad_maximum_fusion.2, s32[1024]{0:T(1024)S(1)} %pad_clamp_fusion.2), kind=kCustom, calls=%fused_computation.10.clone | custom fusion | bytes 8388624 | tf_op jit(solution)/shard_map/jit(_take)/gather | solution.py:54
  342.4 5.0 %gather_fusion.3 = f32[4,2,2,512,128]{4,3,1,2,0:T(8,128)} fusion(f32[2,2,512,4,128]{4,2,0,3,1:T(8,128)} %pad_maximum_fusion.1, s32[1024]{0:T(1024)S(1)} %pad_clamp_fusion.4), kind=kCustom, calls=%fused_computation.2.clone | custom fusion | bytes 8388624 | tf_op jit(solution)/shard_map/jit(_take)/gather | solution.py:54
  347.4 7.9 %bitcast_add_fusion = f32[2,2,512,4,128]{4,2,0,1,3:T(8,128)} fusion(f32[4,2,2,512,128]{4,3,1,2,0:T(8,128)} %gather_fusion.11, f32[4,2,2,512,128]{4,3,1,2,0:T(8,128)} %gather_fusion.7, f32[4,2,2,512,128]{4,3,1,2,0:T(8,128)} %gather_fusion.3, pred[4]{0:T(512)(128)(4,1)S(1)} %get-tuple-element.38, pred[4]{0:T(512)(128)(4,1)S(1)} %get-tuple-element.39, ...), kind=kLoop, calls=%fused_computation.16 | loop fusion | flops 5242880 | bytes 16777228 | tf_op jit(solution)/shard_map/add | solution.py:82
  355.3 5.3 %copy.36 = f32[2,2,512,4,128]{2,4,3,1,0:T(8,128)} copy(f32[2,2,512,4,128]{4,2,0,1,3:T(8,128)} %bitcast_add_fusion) | data formatting | bytes 8388608 | tf_op jit(solution)/shard_map/add | solution.py:82
  360.5 5.2 %copy.37 = f32[1,2,2,512,512]{4,3,2,1,0:T(8,128)} copy(f32[1,2,2,512,512]{3,4,2,1,0:T(8,128)} %bitcast.228) | data formatting | bytes 8388608 | tf_op jit(solution)/shard_map/add | solution.py:82
  (93 shorter events, 63.0 us)
Async XLA Ops:
  0.0 54.1 %copy-start.8 = (bf16[1,2,2,512,512]{4,3,2,1,0:T(8,128)(2,1)S(1)}, bf16[1,2,2,512,512]{4,3,2,1,0:T(8,128)(2,1)}, u32[]{:S(2)}) copy-start(bf16[1,2,2,512,512]{4,3,2,1,0:T(8,128)(2,1)} %param.12) | copy-start | bytes 6291460
  0.0 52.6 %collective-permute-start = (bf16[1,2,2,512,512]{4,3,2,1,0:T(8,128)(2,1)}, bf16[1,2,2,512,512]{4,3,2,1,0:T(8,128)(2,1)S(1)}, u32[]{:S(2)}, u32[]{:S(2)}) collective-permute-start(bf16[1,2,2,512,512]{4,3,2,1,0:T(8,128)(2,1)} %param.12), channel_id=1, source_target_pairs={{0,16},{16,32},{32,48},{48,64},{64,80},{80,96},{96,112},{112,0},{1... | collective-permute-start | bytes 6291464 | tf_op jit(solution)/shard_map/ppermute | solution.py:17
  2.5 53.1 %collective-permute-start.1 = (bf16[1,2,2,512,512]{4,3,2,1,0:T(8,128)(2,1)}, bf16[1,2,2,512,512]{4,3,2,1,0:T(8,128)(2,1)S(1)}, u32[]{:S(2)}, u32[]{:S(2)}) collective-permute-start(bf16[1,2,2,512,512]{4,3,2,1,0:T(8,128)(2,1)} %param.12), channel_id=1, source_target_pairs={{16,0},{32,16},{48,32},{64,48},{80,64},{96,80},{112,96},{0,112},{1... | collective-permute-start | bytes 6291464 | tf_op jit(solution)/shard_map/ppermute | solution.py:20
  55.6 7.1 %copy-start.10 = (s32[3]{0:T(128)S(1)}, s32[3]{0:T(128)}, u32[]{:S(2)}) copy-start(s32[3]{0:T(128)} %param.16) | copy-start | bytes 40
  55.6 10.3 %copy-start.11 = (s32[3]{0:T(128)S(1)}, s32[3]{0:T(128)}, u32[]{:S(2)}) copy-start(s32[3]{0:T(128)} %param.15) | copy-start | bytes 40
  55.6 19.3 %copy-start.12 = (f32[3]{0:T(128)S(1)}, f32[3]{0:T(128)}, u32[]{:S(2)}) copy-start(f32[3]{0:T(128)} %param.17) | copy-start | bytes 40
  55.6 21.9 %copy-start.13 = (s32[3,4,2]{1,2,0:T(2,128)S(1)}, s32[3,4,2]{1,2,0:T(2,128)}, u32[]{:S(2)}) copy-start(s32[3,4,2]{1,2,0:T(2,128)} %param.14) | copy-start | bytes 292
  55.6 22.3 %copy-start.9 = (f32[3,4,2,128,128]{4,3,2,1,0:T(8,128)S(1)}, f32[3,4,2,128,128]{4,3,2,1,0:T(8,128)}, u32[]{:S(2)}) copy-start(f32[3,4,2,128,128]{4,3,2,1,0:T(8,128)} %param.13) | copy-start | bytes 4718596
  57.1 136.5 %collective-permute-start.3 = (bf16[3,2,2,512,512]{4,3,2,1,0:T(8,128)(2,1)}, bf16[3,2,2,512,512]{4,3,2,1,0:T(8,128)(2,1)}, u32[]{:S(2)}, u32[]{:S(2)}) collective-permute-start(bf16[3,2,2,512,512]{4,3,2,1,0:T(8,128)(2,1)} %constant_dynamic-update-slice_fusion), channel_id=1, source_target_pairs={{1,0},{2,1},{3,2},{4,3},{5,4},{6,5},{7,6},{8,7},{9,8},{10,9},{11,1... | collective-permute-start | bytes 18874376 | tf_op jit(solution)/shard_map/ppermute | solution.py:20
  60.2 133.4 %collective-permute-start.2 = (bf16[3,2,2,512,512]{4,3,2,1,0:T(8,128)(2,1)}, bf16[3,2,2,512,512]{4,3,2,1,0:T(8,128)(2,1)}, u32[]{:S(2)}, u32[]{:S(2)}) collective-permute-start(bf16[3,2,2,512,512]{4,3,2,1,0:T(8,128)(2,1)} %constant_dynamic-update-slice_fusion), channel_id=1, source_target_pairs={{0,1},{1,2},{2,3},{3,4},{4,5},{5,6},{6,7},{7,8},{8,9},{9,10},{10,1... | collective-permute-start | bytes 18874376 | tf_op jit(solution)/shard_map/ppermute | solution.py:17
  273.2 3.8 %copy-start = (bf16[2,2,512,4,128]{4,2,0,3,1:T(8,128)(2,1)}, bf16[2,2,512,4,128]{4,2,0,3,1:T(8,128)(2,1)S(1)}, u32[]{:S(2)}) copy-start(bf16[2,2,512,4,128]{4,2,0,3,1:T(8,128)(2,1)S(1)} %fusion.1) | copy-start | bytes 6291460
  313.8 3.8 %copy-start.2 = (bf16[2,2,512,4,128]{4,2,0,3,1:T(8,128)(2,1)}, bf16[2,2,512,4,128]{4,2,0,3,1:T(8,128)(2,1)S(1)}, u32[]{:S(2)}) copy-start(bf16[2,2,512,4,128]{4,2,0,3,1:T(8,128)(2,1)S(1)} %fusion.2) | copy-start | bytes 6291460
  315.9 2.0 copy-start.5
  317.9 1.6 copy-start.4
  322.2 5.1 %copy-start.1 = (bf16[2,2,512,4,128]{4,2,0,3,1:T(8,128)(2,1)S(1)}, bf16[2,2,512,4,128]{4,2,0,3,1:T(8,128)(2,1)}, u32[]{:S(2)}) copy-start(bf16[2,2,512,4,128]{4,2,0,3,1:T(8,128)(2,1)} %copy-done) | copy-start | bytes 6291460
  327.3 2.2 copy-start.6
  332.3 5.1 %copy-start.3 = (bf16[2,2,512,4,128]{4,2,0,3,1:T(8,128)(2,1)S(1)}, bf16[2,2,512,4,128]{4,2,0,3,1:T(8,128)(2,1)}, u32[]{:S(2)}) copy-start(bf16[2,2,512,4,128]{4,2,0,3,1:T(8,128)(2,1)} %copy-done.2) | copy-start | bytes 6291460
  337.5 2.2 copy-start.7
where the time goes:
time: 370 us; the launch traced here: 366 us
  waiting for transfers between devices  161 us (44%)
  local copies, waits for them, and re-layouts  105 us (28%)
  other arithmetic  51.5 us (14%)
  matrix products  22.5 us (6%)
  between operations  13.3 us (4%)
  starting transfers between devices  12.7 us (3%)
    ppermute x2, waiting for transfers between devices, padded(): lax.ppermute(lax.slice_in_dim(block, 0, width, axis=dim), axis, backward)  116 us
    ppermute x2, waiting for transfers between devices, padded(): lax.ppermute(lax.slice_in_dim(block, block.shape[dim] - width, None, axis...  45.5 us
    reshape x6, local copies, waits for them, and re-layouts, sandwich(): left_half.reshape(batch_count, 2, orbitals, block_count, block_size)  20.6 us
    gather x6, local copies, waits for them, and re-layouts, sandwich(): picked = jnp.take(row_blocks, column_index, axis=2)  20.5 us
    dot_general x12, matrix products, product_right(): jnp.einsum('lony,nxy->lonx', other, matrix, preferred_element_type=jnp.fl...  17.3 us
    gather x3, local copies, waits for them, and re-layouts, sandwich(): result = jnp.take(stacked, inverse, axis=3)  15.2 us
    select_n x3, local copies, waits for them, and re-layouts, sandwich(): left_half = jnp.take(products, inverse, axis=2)  10.7 us
    add x2, local copies, waits for them, and re-layouts, on_device(): sigma_sum = sigma_sum + term.reshape(green_lesser.shape)  10.5 us
  transfers between devices with their start and end apart: 4, of which 2 were waited for; matrix products, arithmetic and copies ran while one was open for 1% of the time, Pallas kernels for 0%

commit v1 on v0

v1 whole, which is shorter than its diff:
```python
import jax
import jax.numpy as jnp
from jax import lax
from jax.experimental import pallas as pl
from jax.experimental.pallas import tpu as pltpu
from jax.sharding import PartitionSpec as P

MESH = pl.DeviceIdType.MESH
BS = 128
NB = 4
NCH = NB * NB
F32 = jnp.float32
BF16 = jnp.bfloat16


def pick(flags, values):
    *head, chosen = values
    for flag, value in reversed(list(zip(flags, head))):
        chosen = jnp.where(flag, value, chosen)
    return chosen


def exchange(
    g_hbm, cp_hbm, bl, off, sh, occ,
    in_p, in_m, sc_hbm, tab,
    gbuf, cbuf, ring, wl, wr, sc, sp, sm, snd_p, snd_m, tq, tn, ti, tj, tx, tinv,
    lsem, scsem, s1s, s1r, s2s, s2r, s3s, s3r, s4s, s4r, zps, zpr, zms, zmr,
):
    kz = lax.axis_index("kz")
    en = lax.axis_index("en")
    z = kz % 4
    y = en // 4
    lo = (en // 2) % 2
    c = en % 2
    flip = 2 - 4 * lo
    partner = (kz, en + 1 - 2 * c)
    mate = (kz, en + flip)
    has_y = ((c == 1) & (y < 3)) | ((c == 0) & (y > 0))
    yen = (en + 6 * c - 3 + 16) % 16
    ydev = (kz, yen)
    at_top = (z == 3).astype(jnp.int32)
    at_bot = (z == 0).astype(jnp.int32)
    up = ((kz + 1) % 8, en + flip * at_top)
    down = ((kz + 7) % 8, en + flip * at_bot)

    g_copies = []
    for b in range(NCH):
        rows = pl.ds(b // NB * BS, BS)
        columns = pl.ds(b % NB * BS, BS)
        g_copies.append(pltpu.make_async_copy(g_hbm.at[0, :, :, rows, columns], gbuf.at[b], lsem.at[b]))
        g_copies[b].start()
    c_copy = pltpu.make_async_copy(cp_hbm, cbuf, lsem.at[NCH])
    c_copy.start()

    barrier = pltpu.get_barrier_semaphore()
    for dev in (partner, mate, up, down, ydev):
        pl.semaphore_signal(barrier, inc=1, device_id=dev, device_id_type=MESH)

    o0, o1 = off[0], off[1]
    q_up = jnp.where(o0 == 1, 0, jnp.where(o1 == 1, 1, 2))
    q_dn = jnp.where(o0 == -1, 0, jnp.where(o1 == -1, 1, 2))
    q_th = jnp.maximum(3 - q_up - q_dn, 0)
    qs = (q_up, q_dn, q_th)
    x = off[q_th]
    rho = []
    for s, q in enumerate(qs):
        rows = [bl[q, n, 0] for n in range(NB)]
        cols = [bl[q, n, 1] for n in range(NB)]
        dest = []
        for i in range(NB):
            hit = [cols[n] == i for n in range(NB)]
            tq[s * NB + i] = q
            tn[s * NB + i] = pick(hit, range(NB))
            dest.append(pick(hit, rows))
        rho.append(dest)
    inv = [[pick([rho[s][i] == r for i in range(NB)], range(NB)) for r in range(NB)] for s in range(3)]
    for s in range(3):
        for r in range(NB):
            tinv[s * NB + r] = inv[s][r]
    tau = []
    for i in range(NB):
        r = jnp.where(x == 1, rho[0][i], rho[1][i])
        t = pick([r == a for a in range(NB)], inv[2])
        tau.append(jnp.where(x == 0, i, t))
    ci = jnp.int32(0)
    cj = jnp.int32(0)
    start = jnp.int32(0)
    start_k = jnp.int32(0)
    seen = [jnp.bool_(False)] * NCH
    for k in range(NCH):
        ti[k] = ci
        tj[k] = cj
        cur = ci * NB + cj
        seen = [seen[b] | (cur == b) for b in range(NCH)]
        ni = pick([ci == a for a in range(NB)], tau)
        nj = pick([cj == a for a in range(NB)], tau)
        closing = (ni * NB + nj) == start
        tx[k] = jnp.where(closing, start_k, min(k + 1, NCH - 1))
        if k + 1 < NCH:
            free = jnp.int32(NCH - 1)
            for b in reversed(range(NCH - 1)):
                free = jnp.where(seen[b], free, b)
            fi = free // NB
            ci = jnp.where(closing, fi, ni)
            cj = jnp.where(closing, free - fi * NB, nj)
            start = jnp.where(closing, free, start)
            start_k = jnp.where(closing, k + 1, start_k)

    t_own = 1 + 2 * lo
    t_swp = 3 - 2 * lo

    def c_partner(k):
        return pltpu.make_async_remote_copy(
            ring.at[k, t_own], ring.at[k, 2 * lo + 2 * c], s1s.at[k], s1r.at[k], device_id=partner, device_id_type=MESH)

    def c_mate(k):
        return pltpu.make_async_remote_copy(
            ring.at[k, t_own], ring.at[k, t_own], s2s.at[k], s2r.at[k], device_id=mate, device_id_type=MESH)

    def c_relay(k):
        return pltpu.make_async_remote_copy(
            ring.at[k, t_swp], ring.at[k, 2 - 2 * lo + 2 * c], s3s.at[k], s3r.at[k], device_id=partner, device_id_type=MESH)

    def c_y(k):
        return pltpu.make_async_remote_copy(
            ring.at[k, 1 + 2 * c], ring.at[k, 4 - 4 * c], s4s.at[k], s4r.at[k], device_id=ydev, device_id_type=MESH)

    def c_up(k):
        return pltpu.make_async_remote_copy(
            snd_p.at[k], in_p.at[k], zps.at[k], zpr.at[k], device_id=up, device_id_type=MESH)

    def c_down(k):
        return pltpu.make_async_remote_copy(
            snd_m.at[k], in_m.at[k], zms.at[k], zmr.at[k], device_id=down, device_id_type=MESH)

    def r_partner(k):
        pltpu.make_async_remote_copy(
            ring.at[k, t_own], ring.at[k, 2 * lo + 2 - 2 * c], s1s.at[k], s1r.at[k], device_id=partner, device_id_type=MESH).wait_recv()

    def r_mate(k):
        pltpu.make_async_remote_copy(
            ring.at[k, t_own], ring.at[k, t_swp], s2s.at[k], s2r.at[k], device_id=mate, device_id_type=MESH).wait_recv()

    def r_relay(k):
        pltpu.make_async_remote_copy(
            ring.at[k, t_swp], ring.at[k, 4 - 2 * lo - 2 * c], s3s.at[k], s3r.at[k], device_id=partner, device_id_type=MESH).wait_recv()

    def r_y(k):
        pltpu.make_async_remote_copy(
            ring.at[k, 1 + 2 * c], ring.at[k, 4 * c], s4s.at[k], s4r.at[k], device_id=ydev, device_id_type=MESH).wait_recv()

    def c_sc(k):
        return pltpu.make_async_copy(sc.at[k], sc_hbm.at[k], scsem.at[k])

    for copy in g_copies:
        copy.wait()
    pl.semaphore_wait(barrier, 5)

    @pl.loop(0, NCH)
    def _(k):
        ring[k, t_own] = gbuf[ti[k] * NB + tj[k]]
        c_mate(k).start()
        c_partner(k).start()

    c_copy.wait()

    @pl.loop(0, 3 * NB)
    def _(a):
        block = cbuf[tq[a], tn[a]]
        real, imag = block[0], block[1]
        rb, ib = real.astype(BF16), imag.astype(BF16)
        wl[a, 0:BS, 0:BS] = rb
        wl[a, 0:BS, BS:2 * BS] = -ib
        wl[a, BS:2 * BS, 0:BS] = ib
        wl[a, BS:2 * BS, BS:2 * BS] = rb
        rt, it = real.T.astype(BF16), imag.T.astype(BF16)
        wr[a, 0:BS, 0:BS] = rt
        wr[a, 0:BS, BS:2 * BS] = -it
        wr[a, BS:2 * BS, 0:BS] = it
        wr[a, BS:2 * BS, BS:2 * BS] = rt

    @pl.when(jnp.logical_not(has_y))
    def _():
        @pl.loop(0, NCH)
        def _(k):
            ring[k, 4 * c] = jnp.zeros((2, 2, BS, BS), BF16)

    def relay(k):
        r_mate(k)
        c_relay(k).start()

        @pl.when(has_y)
        def _():
            c_y(k).start()

    relay(0)
    t_up = jnp.where(z == 3, t_swp, t_own)
    t_dn = jnp.where(z == 0, t_swp, t_own)
    w_up = (x == 1).astype(F32)
    w_dn = (x == -1).astype(F32)
    th_swp = ((x == 1) & (z == 3)) | ((x == -1) & (z == 0))

    def sandwich(k, s, six):
        q = qs[s]
        one = sh[q] == 1
        weight = occ[q]
        cols = []
        for e in range(2):
            low = jnp.where(one, six[e + 1], six[e])
            high = jnp.where(one, six[e + 3], six[e + 4])
            mixed = (weight * low.astype(F32) + (weight + 1.0) * high.astype(F32)).astype(BF16)
            cols.append(mixed.reshape(2 * BS, BS))
        field = jnp.concatenate(cols, axis=1)
        left = jnp.dot(wl[s * NB + ti[k]], field, preferred_element_type=F32).astype(BF16)
        top = jnp.concatenate([left[:BS, :BS], left[BS:, :BS]], axis=1)
        bottom = jnp.concatenate([left[:BS, BS:], left[BS:, BS:]], axis=1)
        return jnp.dot(jnp.concatenate([top, bottom], axis=0), wr[s * NB + tj[k]], preferred_element_type=F32)

    def window(k, t):
        return [ring[k, t - 1 + e // 2, e % 2] for e in range(6)]

    def ship(k):
        third = sc[tx[k]]
        snd_p[k] = (sp[...] + w_up * third).astype(BF16)
        snd_m[k] = (sm[...] + w_dn * third).astype(BF16)
        c_up(k).start()
        c_down(k).start()

    @pl.loop(0, NCH)
    def _(k):
        @pl.when(k + 1 < NCH)
        def _():
            relay(k + 1)

        r_partner(k)
        r_relay(k)

        @pl.when(has_y)
        def _():
            r_y(k)

        own = window(k, t_own)
        swp = window(k, t_swp)
        sc[k] = sandwich(k, 2, [jnp.where(th_swp, b, a) for a, b in zip(own, swp)])
        c_sc(k).start()

        @pl.when(k > 0)
        def _():
            ship(k - 1)

        sp[...] = sandwich(k, 0, window(k, t_up))
        sm[...] = sandwich(k, 1, window(k, t_dn))

    ship(NCH - 1)

    @pl.loop(0, NCH)
    def _(d):
        for s in range(3):
            i = tinv[s * NB + d // NB]
            j = tinv[s * NB + d % NB]
            place = 0
            for k in range(NCH):
                place = jnp.where((ti[k] == i) & (tj[k] == j), k, place)
            if s == 2:
                place = jnp.where(x == 0, place, 0)
            tab[s * NCH + d] = place
    tab[3 * NCH] = (x == 0).astype(jnp.int32)

    @pl.loop(0, NCH)
    def _(k):
        c_partner(k).wait_send()
        c_mate(k).wait_send()
        c_relay(k).wait_send()

        @pl.when(has_y)
        def _():
            c_y(k).wait_send()

        c_sc(k).wait()
        c_up(k).wait()
        c_down(k).wait()


def gather_sum(tab, *refs):
    out = refs[-1]
    keep = tab[3 * NCH].astype(F32)
    for j in range(NB):
        total = refs[j][0].astype(F32) + refs[NB + j][0].astype(F32) + keep * refs[2 * NB + j][0]
        for e in range(2):
            for ri in range(2):
                out[0, e, ri, :, j * BS:(j + 1) * BS] = total[e * BS:(e + 1) * BS, ri * BS:(ri + 1) * BS]


def on_device(green_lesser, coupling, block_list, offsets, shifts, occupation):
    any_spec = pl.BlockSpec(memory_space=pl.ANY)
    smem = pl.BlockSpec(memory_space=pltpu.SMEM)
    dma = pltpu.SemaphoreType.DMA
    chunk = (NCH, 2 * BS, 2 * BS)
    in_p, in_m, third, tab = pl.pallas_call(
        exchange,
        out_shape=(
            jax.ShapeDtypeStruct(chunk, BF16),
            jax.ShapeDtypeStruct(chunk, BF16),
            jax.ShapeDtypeStruct(chunk, F32),
            jax.ShapeDtypeStruct((4 * NCH,), jnp.int32),
        ),
        in_specs=[any_spec, any_spec, smem, smem, smem, smem],
        out_specs=(any_spec, any_spec, any_spec, smem),
        scratch_shapes=[
            pltpu.VMEM((NCH, 2, 2, BS, BS), BF16),
            pltpu.VMEM((3, NB, 2, BS, BS), F32),
            pltpu.VMEM((NCH, 5, 2, 2, BS, BS), BF16),
            pltpu.VMEM((3 * NB, 2 * BS, 2 * BS), BF16),
            pltpu.VMEM((3 * NB, 2 * BS, 2 * BS), BF16),
            pltpu.VMEM(chunk, F32),
            pltpu.VMEM((2 * BS, 2 * BS), F32),
            pltpu.VMEM((2 * BS, 2 * BS), F32),
            pltpu.VMEM(chunk, BF16),
            pltpu.VMEM(chunk, BF16),
            pltpu.SMEM((3 * NB,), jnp.int32),
            pltpu.SMEM((3 * NB,), jnp.int32),
            pltpu.SMEM((NCH,), jnp.int32),
            pltpu.SMEM((NCH,), jnp.int32),
            pltpu.SMEM((NCH,), jnp.int32),
            pltpu.SMEM((3 * NB,), jnp.int32),
            dma((NCH + 1,)),
        ] + [dma((NCH,))] * 13,
        compiler_params=pltpu.CompilerParams(
            collective_id=0, has_side_effects=True, vmem_limit_bytes=56 * 1024 * 1024),
        name="exchange",
    )(green_lesser, coupling, block_list, offsets, shifts, occupation)

    def spec(s, j):
        return pl.BlockSpec((1, 2 * BS, 2 * BS), lambda r, t: (t[s * NCH + r * NB + j], 0, 0))

    return pl.pallas_call(
        gather_sum,
        out_shape=jax.ShapeDtypeStruct(green_lesser.shape, F32),
        grid_spec=pltpu.PrefetchScalarGridSpec(
            num_scalar_prefetch=1,
            grid=(NB,),
            in_specs=[spec(s, j) for s in range(3) for j in range(NB)],
            out_specs=pl.BlockSpec((1, 2, 2, BS, 512), lambda r, t: (0, 0, 0, r, 0)),
        ),
        name="gather_sum",
    )(tab, *([in_p] * NB + [in_m] * NB + [third] * NB))


def solution(mesh):
    placed = (P("kz", "en", None, None, None), P(), P(), P(), P(), P())
    return jax.shard_map(
        on_device,
        mesh=mesh,
        in_specs=placed,
        out_specs=P("kz", "en", None, None, None),
        check_vma=False,
    )
```

time: 370 us -> 78.9 us (0.21); the launches traced: 366 us -> 78.6 us
  waiting for transfers between devices: 161 us -> 0 us
  local copies, waits for them, and re-layouts: 105 us -> 1.37 us
  Pallas kernels: 0 us -> 77.2 us
  other arithmetic: 51.5 us -> 0 us
  matrix products: 22.5 us -> 0 us
  between operations: 13.3 us -> 0.01 us
  starting transfers between devices: 12.7 us -> 0 us
    ppermute x4 -> x0, waiting for transfers between devices: 161 us -> none  [the longest x2 116 us: padded(): lax.ppermute(lax.slice_in_dim(block, 0, width, axis=dim), axis, backward)]
    pallas_call x0 -> x2, Pallas kernels: none -> 77.2 us  [the longest x1 70.8 us: on_device(): pl.pallas_call(exchange, out_shape=(jax.ShapeDtypeStruct(chunk, BF16), ja...]
    gather x15 -> x0, local copies, waits for them, and re-layouts: 55 us -> none  [the longest x6 20.5 us: sandwich(): picked = jnp.take(row_blocks, column_index, axis=2)]
    dot_general x24 -> x0, matrix products: 22.5 us -> none  [the longest x12 17.3 us: product_right(): jnp.einsum('lony,nxy->lonx', other, matrix, preferred_element_type=jnp.fl...]
    reshape x6 -> x0, local copies, waits for them, and re-layouts: 20.6 us -> none  [sandwich(): left_half.reshape(batch_count, 2, orbitals, block_count, block_size)]
    select_n x11 -> x0, other arithmetic: 17.8 us -> none  [the longest x3 8.23 us: sandwich(): left_half = jnp.take(products, inverse, axis=2)]
    ppermute x4 -> x0, starting transfers between devices: 12.7 us -> none  [the longest x2 7.79 us: padded(): lax.ppermute(lax.slice_in_dim(block, 0, width, axis=dim), axis, backward)]
    select_n x3 -> x0, local copies, waits for them, and re-layouts: 10.7 us -> none  [sandwich(): left_half = jnp.take(products, inverse, axis=2)]
  transfers between devices with their start and end apart: 4 -> 0, of which waited for: 2 -> 0; matrix products, arithmetic and copies ran while one was open for 1% -> 0% of each run, Pallas kernels for 0% -> 0%
where the time goes in v1:
time: 78.9 us; the launch traced here: 78.6 us
  Pallas kernels  77.2 us (98%)
  local copies, waits for them, and re-layouts  1.37 us (2%)
    pallas_call x1, Pallas kernels, on_device(): pl.pallas_call(exchange, out_shape=(jax.ShapeDtypeStruct(chunk, BF16), ja...  70.8 us
    pallas_call x1, Pallas kernels, on_device(): pl.pallas_call(gather_sum, out_shape=jax.ShapeDtypeStruct(green_lesser.sh...  6.4 us

profile of v1, /device:TPU:1, one launch (start us, length us, event | category | flops | bytes accessed | tf_op | source)
XLA Modules:
  0.0 78.6 jit_solution(8934927126195702802)
XLA Ops:
  0.0 1.4 %copy.7.bl = s32[3,4,2]{2,1,0:T(4,128)} copy(s32[3,4,2]{1,2,0:T(2,128)} %param.8) | data formatting | bytes 192 | tf_op args[2]
  1.4 70.8 %exchange.1 = (bf16[16,256,256]{2,1,0:T(8,128)(2,1)}, bf16[16,256,256]{2,1,0:T(8,128)(2,1)}, f32[16,256,256]{2,1,0:T(8,128)}, s32[64]{0:T(128)}) custom-call(bf16[1,2,2,512,512]{4,3,2,1,0:T(8,128)(2,1)} %g_hbm.1, f32[3,4,2,128,128]{4,3,2,1,0:T(8,128)} %cp_hbm.1, s32[3,4,2]{2,1,0:T(4,128)} %copy.7.bl, s32[3]{0:T(128)} %off.1, s32[3]{0:T(128)} %sh.1, f32[3]{0:T(128)} %occ.1), custom_call_target="tpu_custom_call" | custom-call | tf_op jit(solution)/shard_map/exchange/pallas_call | solution.py:299
  72.2 6.4 %gather_sum.1 = f32[1,2,2,512,512]{4,3,2,1,0:T(8,128)} custom-call(s32[64]{0:T(128)} %get-tuple-element.9.tab, bf16[16,256,256]{2,1,0:T(8,128)(2,1)} %get-tuple-element.10.refs_0_.refs_1_.refs_2_.refs_3_, bf16[16,256,256]{2,1,0:T(8,128)(2,1)} %get-tuple-element.10.refs_0_.refs_1_.refs_2_.refs_3_, ...), custom_call_target="tpu_custom_call" | custom-call | tf_op jit(solution)/shard_map/gather_sum/pallas_call | solution.py:336

commit v2 on v1

--- a/solution.py
+++ b/solution.py
@@ -21,10 +21,10 @@
 
 
 def exchange(
-    g_hbm, cp_hbm, bl, off, sh, occ,
-    in_p, in_m, sc_hbm, tab,
-    gbuf, cbuf, ring, wl, wr, sc, sp, sm, snd_p, snd_m, tq, tn, ti, tj, tx, tinv,
-    lsem, scsem, s1s, s1r, s2s, s2r, s3s, s3r, s4s, s4r, zps, zpr, zms, zmr,
+    g_hbm, cp_hbm, bl_hbm, off_hbm, sh_hbm, occ_hbm,
+    in_p, in_m, sc, tab,
+    gbuf, cbuf, ring, wl, wr, sp, sm, snd_p, snd_m, bl, off, sh, occ, tq, tn, ti, tj, tx, tinv,
+    lsem, isem, s1s, s1r, s2s, s2r, s3s, s3r, s4s, s4r, zps, zpr, zms, zmr,
 ):
     kz = lax.axis_index("kz")
     en = lax.axis_index("en")
@@ -43,18 +43,73 @@
     up = ((kz + 1) % 8, en + flip * at_top)
     down = ((kz + 7) % 8, en + flip * at_bot)
 
+    t_own = 1 + 2 * lo
+    t_swp = 3 - 2 * lo
+    barrier = pltpu.get_barrier_semaphore()
+    for dev in (partner, mate, up, down, ydev):
+        pl.semaphore_signal(barrier, inc=1, device_id=dev, device_id_type=MESH)
     g_copies = []
     for b in range(NCH):
         rows = pl.ds(b // NB * BS, BS)
         columns = pl.ds(b % NB * BS, BS)
-        g_copies.append(pltpu.make_async_copy(g_hbm.at[0, :, :, rows, columns], gbuf.at[b], lsem.at[b]))
+        target = ring.at[0, t_own] if b == 0 else gbuf.at[b]
+        g_copies.append(pltpu.make_async_copy(g_hbm.at[0, :, :, rows, columns], target, lsem.at[b]))
         g_copies[b].start()
+    small = [
+        pltpu.make_async_copy(source, target, isem.at[n])
+        for n, (source, target) in enumerate(((bl_hbm, bl), (off_hbm, off), (sh_hbm, sh), (occ_hbm, occ)))
+    ]
+    for copy in small:
+        copy.start()
     c_copy = pltpu.make_async_copy(cp_hbm, cbuf, lsem.at[NCH])
     c_copy.start()
 
-    barrier = pltpu.get_barrier_semaphore()
-    for dev in (partner, mate, up, down, ydev):
-        pl.semaphore_signal(barrier, inc=1, device_id=dev, device_id_type=MESH)
+    def c_partner(k):
+        return pltpu.make_async_remote_copy(
+            ring.at[k, t_own], ring.at[k, 2 * lo + 2 * c], s1s.at[k], s1r.at[k], device_id=partner, device_id_type=MESH)
+
+    def c_mate(k):
+        return pltpu.make_async_remote_copy(
+            ring.at[k, t_own], ring.at[k, t_own], s2s.at[k], s2r.at[k], device_id=mate, device_id_type=MESH)
+
+    def c_relay(k):
+        return pltpu.make_async_remote_copy(
+            ring.at[k, t_swp], ring.at[k, 2 - 2 * lo + 2 * c], s3s.at[k], s3r.at[k], device_id=partner, device_id_type=MESH)
+
+    def c_y(k):
+        return pltpu.make_async_remote_copy(
+            ring.at[k, 1 + 2 * c], ring.at[k, 4 - 4 * c], s4s.at[k], s4r.at[k], device_id=ydev, device_id_type=MESH)
+
+    def c_up(k):
+        return pltpu.make_async_remote_copy(
+            snd_p.at[k], in_p.at[k], zps.at[k], zpr.at[k], device_id=up, device_id_type=MESH)
+
+    def c_down(k):
+        return pltpu.make_async_remote_copy(
+            snd_m.at[k], in_m.at[k], zms.at[k], zmr.at[k], device_id=down, device_id_type=MESH)
+
+    def r_partner(k):
+        pltpu.make_async_remote_copy(
+            ring.at[k, t_own], ring.at[k, 2 * lo + 2 - 2 * c], s1s.at[k], s1r.at[k], device_id=partner, device_id_type=MESH).wait_recv()
+
+    def r_mate(k):
+        pltpu.make_async_remote_copy(
+            ring.at[k, t_own], ring.at[k, t_swp], s2s.at[k], s2r.at[k], device_id=mate, device_id_type=MESH).wait_recv()
+
+    def r_relay(k):
+        pltpu.make_async_remote_copy(
+            ring.at[k, t_swp], ring.at[k, 4 - 2 * lo - 2 * c], s3s.at[k], s3r.at[k], device_id=partner, device_id_type=MESH).wait_recv()
+
+    def r_y(k):
+        pltpu.make_async_remote_copy(
+            ring.at[k, 1 + 2 * c], ring.at[k, 4 * c], s4s.at[k], s4r.at[k], device_id=ydev, device_id_type=MESH).wait_recv()
+
+    g_copies[0].wait()
+    pl.semaphore_wait(barrier, 5)
+    c_mate(0).start()
+    c_partner(0).start()
+    for copy in small:
+        copy.wait()
 
     o0, o1 = off[0], off[1]
     q_up = jnp.where(o0 == 1, 0, jnp.where(o1 == 1, 1, 2))
@@ -64,8 +119,8 @@
     x = off[q_th]
     rho = []
     for s, q in enumerate(qs):
-        rows = [bl[q, n, 0] for n in range(NB)]
-        cols = [bl[q, n, 1] for n in range(NB)]
+        rows = [bl[q, 0, n] for n in range(NB)]
+        cols = [bl[q, 1, n] for n in range(NB)]
         dest = []
         for i in range(NB):
             hit = [cols[n] == i for n in range(NB)]
@@ -106,57 +161,10 @@
             start = jnp.where(closing, free, start)
             start_k = jnp.where(closing, k + 1, start_k)
 
-    t_own = 1 + 2 * lo
-    t_swp = 3 - 2 * lo
-
-    def c_partner(k):
-        return pltpu.make_async_remote_copy(
-            ring.at[k, t_own], ring.at[k, 2 * lo + 2 * c], s1s.at[k], s1r.at[k], device_id=partner, device_id_type=MESH)
-
-    def c_mate(k):
-        return pltpu.make_async_remote_copy(
-            ring.at[k, t_own], ring.at[k, t_own], s2s.at[k], s2r.at[k], device_id=mate, device_id_type=MESH)
-
-    def c_relay(k):
-        return pltpu.make_async_remote_copy(
-            ring.at[k, t_swp], ring.at[k, 2 - 2 * lo + 2 * c], s3s.at[k], s3r.at[k], device_id=partner, device_id_type=MESH)
-
-    def c_y(k):
-        return pltpu.make_async_remote_copy(
-            ring.at[k, 1 + 2 * c], ring.at[k, 4 - 4 * c], s4s.at[k], s4r.at[k], device_id=ydev, device_id_type=MESH)
-
-    def c_up(k):
-        return pltpu.make_async_remote_copy(
-            snd_p.at[k], in_p.at[k], zps.at[k], zpr.at[k], device_id=up, device_id_type=MESH)
-
-    def c_down(k):
-        return pltpu.make_async_remote_copy(
-            snd_m.at[k], in_m.at[k], zms.at[k], zmr.at[k], device_id=down, device_id_type=MESH)
-
-    def r_partner(k):
-        pltpu.make_async_remote_copy(
-            ring.at[k, t_own], ring.at[k, 2 * lo + 2 - 2 * c], s1s.at[k], s1r.at[k], device_id=partner, device_id_type=MESH).wait_recv()
-
-    def r_mate(k):
-        pltpu.make_async_remote_copy(
-            ring.at[k, t_own], ring.at[k, t_swp], s2s.at[k], s2r.at[k], device_id=mate, device_id_type=MESH).wait_recv()
-
-    def r_relay(k):
-        pltpu.make_async_remote_copy(
-            ring.at[k, t_swp], ring.at[k, 4 - 2 * lo - 2 * c], s3s.at[k], s3r.at[k], device_id=partner, device_id_type=MESH).wait_recv()
-
-    def r_y(k):
-        pltpu.make_async_remote_copy(
-            ring.at[k, 1 + 2 * c], ring.at[k, 4 * c], s4s.at[k], s4r.at[k], device_id=ydev, device_id_type=MESH).wait_recv()
-
-    def c_sc(k):
-        return pltpu.make_async_copy(sc.at[k], sc_hbm.at[k], scsem.at[k])
-
-    for copy in g_copies:
+    for copy in g_copies[1:]:
         copy.wait()
-    pl.semaphore_wait(barrier, 5)
-
-    @pl.loop(0, NCH)
+
+    @pl.loop(1, NCH)
     def _(k):
         ring[k, t_own] = gbuf[ti[k] * NB + tj[k]]
         c_mate(k).start()
@@ -242,7 +250,6 @@
         own = window(k, t_own)
         swp = window(k, t_swp)
         sc[k] = sandwich(k, 2, [jnp.where(th_swp, b, a) for a, b in zip(own, swp)])
-        c_sc(k).start()
 
         @pl.when(k > 0)
         def _():
@@ -276,47 +283,74 @@
         def _():
             c_y(k).wait_send()
 
-        c_sc(k).wait()
-        c_up(k).wait()
-        c_down(k).wait()
-
-
-def gather_sum(tab, *refs):
-    out = refs[-1]
-    keep = tab[3 * NCH].astype(F32)
-    for j in range(NB):
-        total = refs[j][0].astype(F32) + refs[NB + j][0].astype(F32) + keep * refs[2 * NB + j][0]
-        for e in range(2):
-            for ri in range(2):
-                out[0, e, ri, :, j * BS:(j + 1) * BS] = total[e * BS:(e + 1) * BS, ri * BS:(ri + 1) * BS]
+        c_up(k).wait_send()
+        c_down(k).wait_send()
+
+    @pl.loop(0, NCH)
+    def _(k):
+        c_up(k).wait_recv()
+        c_down(k).wait_recv()
+
+
+def gather_sum(tab, in_p, in_m, third, out, rows, sem):
+    def copy(r):
+        return pltpu.make_async_copy(rows.at[r], out.at[0, :, :, pl.ds(r * BS, BS), :], sem.at[r])
+
+    def fill(own):
+        for r in range(NB):
+            for j in range(NB):
+                d = r * NB + j
+                total = in_p[tab[d]].astype(F32) + in_m[tab[NCH + d]].astype(F32)
+                if own:
+                    total = total + third[tab[2 * NCH + d]]
+                for e in range(2):
+                    for ri in range(2):
+                        rows[r, e, ri, :, j * BS:(j + 1) * BS] = total[e * BS:(e + 1) * BS, ri * BS:(ri + 1) * BS]
+            copy(r).start()
+
+    @pl.when(tab[3 * NCH] == 1)
+    def _():
+        fill(True)
+
+    @pl.when(tab[3 * NCH] != 1)
+    def _():
+        fill(False)
+
+    for r in range(NB):
+        copy(r).wait()
 
 
 def on_device(green_lesser, coupling, block_list, offsets, shifts, occupation):
     any_spec = pl.BlockSpec(memory_space=pl.ANY)
+    hbm = pl.BlockSpec(memory_space=pltpu.HBM)
     smem = pl.BlockSpec(memory_space=pltpu.SMEM)
+    vmem = pl.BlockSpec(memory_space=pltpu.VMEM)
     dma = pltpu.SemaphoreType.DMA
     chunk = (NCH, 2 * BS, 2 * BS)
     in_p, in_m, third, tab = pl.pallas_call(
         exchange,
         out_shape=(
-            jax.ShapeDtypeStruct(chunk, BF16),
-            jax.ShapeDtypeStruct(chunk, BF16),
-            jax.ShapeDtypeStruct(chunk, F32),
-            jax.ShapeDtypeStruct((4 * NCH,), jnp.int32),
+            pltpu.VMEM(chunk, BF16),
+            pltpu.VMEM(chunk, BF16),
+            pltpu.VMEM(chunk, F32),
+            pltpu.SMEM((4 * NCH,), jnp.int32),
         ),
-        in_specs=[any_spec, any_spec, smem, smem, smem, smem],
-        out_specs=(any_spec, any_spec, any_spec, smem),
+        in_specs=[hbm] * 6,
+        out_specs=(vmem, vmem, vmem, smem),
         scratch_shapes=[
             pltpu.VMEM((NCH, 2, 2, BS, BS), BF16),
             pltpu.VMEM((3, NB, 2, BS, BS), F32),
             pltpu.VMEM((NCH, 5, 2, 2, BS, BS), BF16),
             pltpu.VMEM((3 * NB, 2 * BS, 2 * BS), BF16),
             pltpu.VMEM((3 * NB, 2 * BS, 2 * BS), BF16),
-            pltpu.VMEM(chunk, F32),
             pltpu.VMEM((2 * BS, 2 * BS), F32),
             pltpu.VMEM((2 * BS, 2 * BS), F32),
             pltpu.VMEM(chunk, BF16),
             pltpu.VMEM(chunk, BF16),
+            pltpu.SMEM((3, 2, NB), jnp.int32),
+            pltpu.SMEM((3,), jnp.int32),
+            pltpu.SMEM((3,), jnp.int32),
+            pltpu.SMEM((3,), F32),
             pltpu.SMEM((3 * NB,), jnp.int32),
             pltpu.SMEM((3 * NB,), jnp.int32),
             pltpu.SMEM((NCH,), jnp.int32),
@@ -324,26 +358,24 @@
             pltpu.SMEM((NCH,), jnp.int32),
             pltpu.SMEM((3 * NB,), jnp.int32),
             dma((NCH + 1,)),
-        ] + [dma((NCH,))] * 13,
+            dma((4,)),
+        ] + [dma((NCH,))] * 12,
         compiler_params=pltpu.CompilerParams(
-            collective_id=0, has_side_effects=True, vmem_limit_bytes=56 * 1024 * 1024),
+            collective_id=0, has_side_effects=True, vmem_limit_bytes=32 * 1024 * 1024),
         name="exchange",
-    )(green_lesser, coupling, block_list, offsets, shifts, occupation)
-
-    def spec(s, j):
-        return pl.BlockSpec((1, 2 * BS, 2 * BS), lambda r, t: (t[s * NCH + r * NB + j], 0, 0))
-
+    )(*(
+        pltpu.with_memory_space_constraint(x, pltpu.HBM)
+        for x in (green_lesser, coupling, block_list.transpose(0, 2, 1), offsets, shifts, occupation)
+    ))
     return pl.pallas_call(
         gather_sum,
         out_shape=jax.ShapeDtypeStruct(green_lesser.shape, F32),
-        grid_spec=pltpu.PrefetchScalarGridSpec(
-            num_scalar_prefetch=1,
-            grid=(NB,),
-            in_specs=[spec(s, j) for s in range(3) for j in range(NB)],
-            out_specs=pl.BlockSpec((1, 2, 2, BS, 512), lambda r, t: (0, 0, 0, r, 0)),
-        ),
+        in_specs=[smem, vmem, vmem, vmem],
+        out_specs=any_spec,
+        scratch_shapes=[pltpu.VMEM((NB, 2, 2, BS, 512), F32), dma((NB,))],
+        compiler_params=pltpu.CompilerParams(vmem_limit_bytes=16 * 1024 * 1024),
         name="gather_sum",
-    )(tab, *([in_p] * NB + [in_m] * NB + [third] * NB))
+    )(tab, in_p, in_m, third)
 
 
 def solution(mesh):

time: 78.9 us -> 71.6 us (0.907)
  Pallas kernels: 77.2 us -> 71.5 us
  local copies, waits for them, and re-layouts: 1.37 us -> 0 us
    pallas_call x1, Pallas kernels: 6.4 us -> 2.21 us  [on_device(): pl.pallas_call(gather_sum, out_shape=jax.ShapeDtypeStruct(green_lesser.sh...]
    pallas_call x1, Pallas kernels: 70.8 us -> 69.3 us  [on_device(): pl.pallas_call(exchange, out_shape=(pltpu.VMEM(chunk, BF16), pltpu.VMEM(c...]
    unnamed x1 -> x0, local copies, waits for them, and re-layouts: 1.37 us -> none
where the time goes in v2:
time: 71.6 us; the launch traced here: 71.5 us
  Pallas kernels  71.5 us (100%)
    pallas_call x1, Pallas kernels, on_device(): pl.pallas_call(exchange, out_shape=(pltpu.VMEM(chunk, BF16), pltpu.VMEM(c...  69.3 us
    pallas_call x1, Pallas kernels, on_device(): pl.pallas_call(gather_sum, out_shape=jax.ShapeDtypeStruct(green_lesser.sh...  2.21 us

profile of v2, /device:TPU:1, one launch (start us, length us, event | category | flops | bytes accessed | tf_op | source)
XLA Modules:
  0.0 71.5 jit_solution(824854204317376837)
XLA Ops:
  0.0 69.3 %exchange.1 = (bf16[16,256,256]{2,1,0:T(8,128)(2,1)S(1)}, bf16[16,256,256]{2,1,0:T(8,128)(2,1)S(1)}, f32[16,256,256]{2,1,0:T(8,128)S(1)}, s32[64]{0:T(128)S(4)}) custom-call(bf16[1,2,2,512,512]{4,3,2,1,0:T(8,128)(2,1)} %g_hbm.1, f32[3,4,2,128,128]{4,3,2,1,0:T(8,128)} %cp_hbm.1, s32[3,2,4]{2,1,0:T(2,128)} %bitcast.1, s32[3]{0:T(128)} %off_hbm.1, s32[3]{0:T(128)} %sh_hbm.1, ...), custom_call_target="tpu_custom_call" | custom-call | tf_op jit(solution)/shard_map/exchange/pallas_call | solution.py:330
  69.3 2.2 %gather_sum.1 = f32[1,2,2,512,512]{4,3,2,1,0:T(8,128)} custom-call(s32[64]{0:T(128)S(4)} %get-tuple-element.9.tab, bf16[16,256,256]{2,1,0:T(8,128)(2,1)S(1)} %get-tuple-element.10.in_p, bf16[16,256,256]{2,1,0:T(8,128)(2,1)S(1)} %get-tuple-element.11.in_m, f32[16,256,256]{2,1,0:T(8,128)S(1)} %get-tuple-element.12.third), custom_call_target="tpu_custom_call" | custom-call | tf_op jit(solution)/shard_map/gather_sum/pallas_call | solution.py:370

commit v3 on v2

--- a/solution.py
+++ b/solution.py
@@ -24,7 +24,7 @@
     g_hbm, cp_hbm, bl_hbm, off_hbm, sh_hbm, occ_hbm,
     in_p, in_m, sc, tab,
     gbuf, cbuf, ring, wl, wr, sp, sm, snd_p, snd_m, bl, off, sh, occ, tq, tn, ti, tj, tx, tinv,
-    lsem, isem, s1s, s1r, s2s, s2r, s3s, s3r, s4s, s4r, zps, zpr, zms, zmr,
+    lsem, isem, sent, got, s1r, s2r, s3r, s4r,
 ):
     kz = lax.axis_index("kz")
     en = lax.axis_index("en")
@@ -45,69 +45,84 @@
 
     t_own = 1 + 2 * lo
     t_swp = 3 - 2 * lo
-    barrier = pltpu.get_barrier_semaphore()
-    for dev in (partner, mate, up, down, ydev):
-        pl.semaphore_signal(barrier, inc=1, device_id=dev, device_id_type=MESH)
-    g_copies = []
-    for b in range(NCH):
+    def g_copy(b):
         rows = pl.ds(b // NB * BS, BS)
         columns = pl.ds(b % NB * BS, BS)
         target = ring.at[0, t_own] if b == 0 else gbuf.at[b]
-        g_copies.append(pltpu.make_async_copy(g_hbm.at[0, :, :, rows, columns], target, lsem.at[b]))
-        g_copies[b].start()
+        return pltpu.make_async_copy(g_hbm.at[0, :, :, rows, columns], target, lsem.at[min(b, 1)])
+
+    g_copy(0).start()
+    barrier = pltpu.get_barrier_semaphore()
+    for dev in (up, down, ydev, mate, partner):
+        pl.semaphore_signal(barrier, inc=1, device_id=dev, device_id_type=MESH)
     small = [
         pltpu.make_async_copy(source, target, isem.at[n])
         for n, (source, target) in enumerate(((bl_hbm, bl), (off_hbm, off), (sh_hbm, sh), (occ_hbm, occ)))
     ]
     for copy in small:
         copy.start()
-    c_copy = pltpu.make_async_copy(cp_hbm, cbuf, lsem.at[NCH])
+    c_copy = pltpu.make_async_copy(cp_hbm, cbuf, lsem.at[2])
+
+    def c_partner(k, sem):
+        return pltpu.make_async_remote_copy(
+            ring.at[k, t_own], ring.at[k, 2 * lo + 2 * c], sent.at[0], s1r.at[sem],
+            device_id=partner, device_id_type=MESH)
+
+    def c_mate(k):
+        return pltpu.make_async_remote_copy(
+            ring.at[k, t_own], ring.at[k, t_own], sent.at[1], s2r.at[k], device_id=mate, device_id_type=MESH)
+
+    def c_relay(k):
+        return pltpu.make_async_remote_copy(
+            ring.at[k, t_swp], ring.at[k, 2 - 2 * lo + 2 * c], sent.at[2], s3r.at[k],
+            device_id=partner, device_id_type=MESH)
+
+    def c_y(k):
+        return pltpu.make_async_remote_copy(
+            ring.at[k, 1 + 2 * c], ring.at[k, 4 - 4 * c], sent.at[3], s4r.at[k], device_id=ydev, device_id_type=MESH)
+
+    def c_up(k):
+        return pltpu.make_async_remote_copy(
+            snd_p.at[k], in_p.at[k], sent.at[4], got.at[0], device_id=up, device_id_type=MESH)
+
+    def c_down(k):
+        return pltpu.make_async_remote_copy(
+            snd_m.at[k], in_m.at[k], sent.at[5], got.at[1], device_id=down, device_id_type=MESH)
+
+    def arrived(target, sem, device):
+        pltpu.make_async_remote_copy(
+            target, target, sent.at[0], sem, device_id=device, device_id_type=MESH).wait_recv()
+
+    def r_mate(k):
+        arrived(ring.at[k, t_swp], s2r.at[k], mate)
+
+    def r_relay(k):
+        arrived(ring.at[k, 4 - 2 * lo - 2 * c], s3r.at[k], partner)
+
+    def r_y(k):
+        arrived(ring.at[k, 4 * c], s4r.at[k], ydev)
+
+    t_partner = 2 * lo + 2 - 2 * c
+    y_own = has_y & (lo == c)
+    y_relay = has_y & (lo != c)
+
+    def send_mate(k):
+        c_mate(k).start()
+
+    def send_chip(k, sem):
+        c_partner(k, sem).start()
+
+        @pl.when(y_own)
+        def _():
+            c_y(k).start()
+
+    g_copy(0).wait()
+    pl.semaphore_wait(barrier, 5)
+    send_mate(0)
+    send_chip(0, 0)
+    for b in range(1, NCH):
+        g_copy(b).start()
     c_copy.start()
-
-    def c_partner(k):
-        return pltpu.make_async_remote_copy(
-            ring.at[k, t_own], ring.at[k, 2 * lo + 2 * c], s1s.at[k], s1r.at[k], device_id=partner, device_id_type=MESH)
-
-    def c_mate(k):
-        return pltpu.make_async_remote_copy(
-            ring.at[k, t_own], ring.at[k, t_own], s2s.at[k], s2r.at[k], device_id=mate, device_id_type=MESH)
-
-    def c_relay(k):
-        return pltpu.make_async_remote_copy(
-            ring.at[k, t_swp], ring.at[k, 2 - 2 * lo + 2 * c], s3s.at[k], s3r.at[k], device_id=partner, device_id_type=MESH)
-
-    def c_y(k):
-        return pltpu.make_async_remote_copy(
-            ring.at[k, 1 + 2 * c], ring.at[k, 4 - 4 * c], s4s.at[k], s4r.at[k], device_id=ydev, device_id_type=MESH)
-
-    def c_up(k):
-        return pltpu.make_async_remote_copy(
-            snd_p.at[k], in_p.at[k], zps.at[k], zpr.at[k], device_id=up, device_id_type=MESH)
-
-    def c_down(k):
-        return pltpu.make_async_remote_copy(
-            snd_m.at[k], in_m.at[k], zms.at[k], zmr.at[k], device_id=down, device_id_type=MESH)
-
-    def r_partner(k):
-        pltpu.make_async_remote_copy(
-            ring.at[k, t_own], ring.at[k, 2 * lo + 2 - 2 * c], s1s.at[k], s1r.at[k], device_id=partner, device_id_type=MESH).wait_recv()
-
-    def r_mate(k):
-        pltpu.make_async_remote_copy(
-            ring.at[k, t_own], ring.at[k, t_swp], s2s.at[k], s2r.at[k], device_id=mate, device_id_type=MESH).wait_recv()
-
-    def r_relay(k):
-        pltpu.make_async_remote_copy(
-            ring.at[k, t_swp], ring.at[k, 4 - 2 * lo - 2 * c], s3s.at[k], s3r.at[k], device_id=partner, device_id_type=MESH).wait_recv()
-
-    def r_y(k):
-        pltpu.make_async_remote_copy(
-            ring.at[k, 1 + 2 * c], ring.at[k, 4 * c], s4s.at[k], s4r.at[k], device_id=ydev, device_id_type=MESH).wait_recv()
-
-    g_copies[0].wait()
-    pl.semaphore_wait(barrier, 5)
-    c_mate(0).start()
-    c_partner(0).start()
     for copy in small:
         copy.wait()
 
@@ -161,14 +176,27 @@
             start = jnp.where(closing, free, start)
             start_k = jnp.where(closing, k + 1, start_k)
 
-    for copy in g_copies[1:]:
-        copy.wait()
+    others = gbuf.at[pl.ds(1, NCH - 1)]
+    pltpu.make_async_copy(others, others, lsem.at[1]).wait()
 
     @pl.loop(1, NCH)
     def _(k):
         ring[k, t_own] = gbuf[ti[k] * NB + tj[k]]
-        c_mate(k).start()
-        c_partner(k).start()
+
+        @pl.when(lo == c)
+        def _():
+            send_mate(k)
+
+        send_chip(k, 1)
+
+    arrived(ring.at[0, t_partner], s1r.at[0], partner)
+    arrived(ring.at[pl.ds(1, NCH - 1), t_partner], s1r.at[1], partner)
+
+    @pl.when(lo != c)
+    def _():
+        @pl.loop(1, NCH)
+        def _(k):
+            send_mate(k)
 
     c_copy.wait()
 
@@ -195,13 +223,15 @@
 
     def relay(k):
         r_mate(k)
+
+        @pl.when(y_relay)
+        def _():
+            c_y(k).start()
+
         c_relay(k).start()
 
-        @pl.when(has_y)
-        def _():
-            c_y(k).start()
-
     relay(0)
+
     t_up = jnp.where(z == 3, t_swp, t_own)
     t_dn = jnp.where(z == 0, t_swp, t_own)
     w_up = (x == 1).astype(F32)
@@ -240,7 +270,6 @@
         def _():
             relay(k + 1)
 
-        r_partner(k)
         r_relay(k)
 
         @pl.when(has_y)
@@ -273,23 +302,19 @@
             tab[s * NCH + d] = place
     tab[3 * NCH] = (x == 0).astype(jnp.int32)
 
-    @pl.loop(0, NCH)
-    def _(k):
-        c_partner(k).wait_send()
-        c_mate(k).wait_send()
-        c_relay(k).wait_send()
-
-        @pl.when(has_y)
-        def _():
-            c_y(k).wait_send()
-
-        c_up(k).wait_send()
-        c_down(k).wait_send()
-
-    @pl.loop(0, NCH)
-    def _(k):
-        c_up(k).wait_recv()
-        c_down(k).wait_recv()
+    def all_sent(n):
+        pltpu.make_async_remote_copy(
+            snd_p, snd_p, sent.at[n], got.at[0], device_id=partner, device_id_type=MESH).wait_send()
+
+    for n in (0, 1, 2, 4, 5):
+        all_sent(n)
+
+    @pl.when(has_y)
+    def _():
+        all_sent(3)
+
+    arrived(in_p, got.at[0], up)
+    arrived(in_m, got.at[1], down)
 
 
 def gather_sum(tab, in_p, in_m, third, out, rows, sem):
@@ -357,9 +382,15 @@
             pltpu.SMEM((NCH,), jnp.int32),
             pltpu.SMEM((NCH,), jnp.int32),
             pltpu.SMEM((3 * NB,), jnp.int32),
-            dma((NCH + 1,)),
+            dma((3,)),
             dma((4,)),
-        ] + [dma((NCH,))] * 12,
+            dma((6,)),
+            dma((2,)),
+            dma((2,)),
+            dma((NCH,)),
+            dma((NCH,)),
+            dma((NCH,)),
+        ],
         compiler_params=pltpu.CompilerParams(
             collective_id=0, has_side_effects=True, vmem_limit_bytes=32 * 1024 * 1024),
         name="exchange",

time: 71.6 us -> 70.4 us (0.983)
  Pallas kernels: 71.5 us -> 70.3 us
    pallas_call x1, Pallas kernels: 69.3 us -> 68.1 us  [on_device(): pl.pallas_call(exchange, out_shape=(pltpu.VMEM(chunk, BF16), pltpu.VMEM(c...]
where the time goes in v3:
time: 70.4 us; the launch traced here: 70.3 us
  Pallas kernels  70.3 us (100%)
    pallas_call x1, Pallas kernels, on_device(): pl.pallas_call(exchange, out_shape=(pltpu.VMEM(chunk, BF16), pltpu.VMEM(c...  68.1 us
    pallas_call x1, Pallas kernels, on_device(): pl.pallas_call(gather_sum, out_shape=jax.ShapeDtypeStruct(green_lesser.sh...  2.21 us

profile of v3, /device:TPU:1, one launch (start us, length us, event | category | flops | bytes accessed | tf_op | source)
XLA Modules:
  0.0 70.3 jit_solution(17199596912554652847)
XLA Ops:
  0.0 68.1 %exchange.1 = (bf16[16,256,256]{2,1,0:T(8,128)(2,1)S(1)}, bf16[16,256,256]{2,1,0:T(8,128)(2,1)S(1)}, f32[16,256,256]{2,1,0:T(8,128)S(1)}, s32[64]{0:T(128)S(4)}) custom-call(bf16[1,2,2,512,512]{4,3,2,1,0:T(8,128)(2,1)} %g_hbm.1, f32[3,4,2,128,128]{4,3,2,1,0:T(8,128)} %cp_hbm.1, s32[3,2,4]{2,1,0:T(2,128)} %bitcast.1, s32[3]{0:T(128)} %off_hbm.1, s32[3]{0:T(128)} %sh_hbm.1, ...), custom_call_target="tpu_custom_call" | custom-call | tf_op jit(solution)/shard_map/exchange/pallas_call | solution.py:355
  68.1 2.2 %gather_sum.1 = f32[1,2,2,512,512]{4,3,2,1,0:T(8,128)} custom-call(s32[64]{0:T(128)S(4)} %get-tuple-element.9.tab, bf16[16,256,256]{2,1,0:T(8,128)(2,1)S(1)} %get-tuple-element.10.in_p, bf16[16,256,256]{2,1,0:T(8,128)(2,1)S(1)} %get-tuple-element.11.in_m, f32[16,256,256]{2,1,0:T(8,128)S(1)} %get-tuple-element.12.third), custom_call_target="tpu_custom_call" | custom-call | tf_op jit(solution)/shard_map/gather_sum/pallas_call | solution.py:401

commit v4 on v3

--- a/solution.py
+++ b/solution.py
@@ -24,7 +24,7 @@
     g_hbm, cp_hbm, bl_hbm, off_hbm, sh_hbm, occ_hbm,
     in_p, in_m, sc, tab,
     gbuf, cbuf, ring, wl, wr, sp, sm, snd_p, snd_m, bl, off, sh, occ, tq, tn, ti, tj, tx, tinv,
-    lsem, isem, sent, got, s1r, s2r, s3r, s4r,
+    ready, lsem, isem, sent, got, s1r, s2r, s3r, s4r,
 ):
     kz = lax.axis_index("kz")
     en = lax.axis_index("en")
@@ -53,7 +53,16 @@
 
     g_copy(0).start()
     barrier = pltpu.get_barrier_semaphore()
-    for dev in (up, down, ydev, mate, partner):
+
+    @pl.when(z < 3)
+    def _():
+        pl.semaphore_signal(barrier, inc=1, device_id=up, device_id_type=MESH)
+
+    @pl.when(z == 0)
+    def _():
+        pl.semaphore_signal(barrier, inc=1, device_id=down, device_id_type=MESH)
+
+    for dev in (ydev, mate, partner):
         pl.semaphore_signal(barrier, inc=1, device_id=dev, device_id_type=MESH)
     small = [
         pltpu.make_async_copy(source, target, isem.at[n])
@@ -117,9 +126,18 @@
             c_y(k).start()
 
     g_copy(0).wait()
-    pl.semaphore_wait(barrier, 5)
+    pl.semaphore_wait(barrier, 3 + (z > 0).astype(jnp.int32) + at_top)
     send_mate(0)
     send_chip(0, 0)
+
+    @pl.when(z > 0)
+    def _():
+        pl.semaphore_signal(ready.at[0], inc=1, device_id=down, device_id_type=MESH)
+
+    @pl.when(z == 3)
+    def _():
+        pl.semaphore_signal(ready.at[1], inc=1, device_id=up, device_id_type=MESH)
+
     for b in range(1, NCH):
         g_copy(b).start()
     c_copy.start()
@@ -183,20 +201,12 @@
     def _(k):
         ring[k, t_own] = gbuf[ti[k] * NB + tj[k]]
 
-        @pl.when(lo == c)
-        def _():
-            send_mate(k)
-
+        send_mate(k)
         send_chip(k, 1)
 
     arrived(ring.at[0, t_partner], s1r.at[0], partner)
     arrived(ring.at[pl.ds(1, NCH - 1), t_partner], s1r.at[1], partner)
 
-    @pl.when(lo != c)
-    def _():
-        @pl.loop(1, NCH)
-        def _(k):
-            send_mate(k)
 
     c_copy.wait()
 
@@ -279,6 +289,14 @@
         own = window(k, t_own)
         swp = window(k, t_swp)
         sc[k] = sandwich(k, 2, [jnp.where(th_swp, b, a) for a, b in zip(own, swp)])
+
+        @pl.when((k == 1) & (z < 3))
+        def _():
+            pl.semaphore_wait(ready.at[0], 1)
+
+        @pl.when((k == 1) & (z == 0))
+        def _():
+            pl.semaphore_wait(ready.at[1], 1)
 
         @pl.when(k > 0)
         def _():
@@ -382,6 +400,7 @@
             pltpu.SMEM((NCH,), jnp.int32),
             pltpu.SMEM((NCH,), jnp.int32),
             pltpu.SMEM((3 * NB,), jnp.int32),
+            pltpu.SemaphoreType.REGULAR((2,)),
             dma((3,)),
             dma((4,)),
             dma((6,)),

time: 70.4 us -> 70.2 us (level)
  no operation moved by 1% of the time
where the time goes in v4:
time: 70.2 us; the launch traced here: 70.1 us
  Pallas kernels  70.1 us (100%)
    pallas_call x1, Pallas kernels, on_device(): pl.pallas_call(exchange, out_shape=(pltpu.VMEM(chunk, BF16), pltpu.VMEM(c...  67.9 us
    pallas_call x1, Pallas kernels, on_device(): pl.pallas_call(gather_sum, out_shape=jax.ShapeDtypeStruct(green_lesser.sh...  2.21 us

profile of v4, /device:TPU:1, one launch (start us, length us, event | category | flops | bytes accessed | tf_op | source)
XLA Modules:
  0.0 70.1 jit_solution(8579390584521460639)
XLA Ops:
  0.0 67.9 %exchange.1 = (bf16[16,256,256]{2,1,0:T(8,128)(2,1)S(1)}, bf16[16,256,256]{2,1,0:T(8,128)(2,1)S(1)}, f32[16,256,256]{2,1,0:T(8,128)S(1)}, s32[64]{0:T(128)S(4)}) custom-call(bf16[1,2,2,512,512]{4,3,2,1,0:T(8,128)(2,1)} %g_hbm.1, f32[3,4,2,128,128]{4,3,2,1,0:T(8,128)} %cp_hbm.1, s32[3,2,4]{2,1,0:T(2,128)} %bitcast.1, s32[3]{0:T(128)} %off_hbm.1, s32[3]{0:T(128)} %sh_hbm.1, ...), custom_call_target="tpu_custom_call" | custom-call | tf_op jit(solution)/shard_map/exchange/pallas_call | solution.py:373
  67.9 2.2 %gather_sum.1 = f32[1,2,2,512,512]{4,3,2,1,0:T(8,128)} custom-call(s32[64]{0:T(128)S(4)} %get-tuple-element.9.tab, bf16[16,256,256]{2,1,0:T(8,128)(2,1)S(1)} %get-tuple-element.10.in_p, bf16[16,256,256]{2,1,0:T(8,128)(2,1)S(1)} %get-tuple-element.11.in_m, f32[16,256,256]{2,1,0:T(8,128)S(1)} %get-tuple-element.12.third), custom_call_target="tpu_custom_call" | custom-call | tf_op jit(solution)/shard_map/gather_sum/pallas_call | solution.py:420

commit v5 on v4

--- a/solution.py
+++ b/solution.py
@@ -204,10 +204,17 @@
         send_mate(k)
         send_chip(k, 1)
 
-    arrived(ring.at[0, t_partner], s1r.at[0], partner)
-    arrived(ring.at[pl.ds(1, NCH - 1), t_partner], s1r.at[1], partner)
-
-
+
+    def relay(k):
+        r_mate(k)
+
+        @pl.when(y_relay)
+        def _():
+            c_y(k).start()
+
+        c_relay(k).start()
+
+    relay(0)
     c_copy.wait()
 
     @pl.loop(0, 3 * NB)
@@ -231,16 +238,6 @@
         def _(k):
             ring[k, 4 * c] = jnp.zeros((2, 2, BS, BS), BF16)
 
-    def relay(k):
-        r_mate(k)
-
-        @pl.when(y_relay)
-        def _():
-            c_y(k).start()
-
-        c_relay(k).start()
-
-    relay(0)
 
     t_up = jnp.where(z == 3, t_swp, t_own)
     t_dn = jnp.where(z == 0, t_swp, t_own)
@@ -270,8 +267,8 @@
     def ship(k):
         third = sc[tx[k]]
         snd_p[k] = (sp[...] + w_up * third).astype(BF16)
+        c_up(k).start()
         snd_m[k] = (sm[...] + w_dn * third).astype(BF16)
-        c_up(k).start()
         c_down(k).start()
 
     @pl.loop(0, NCH)
@@ -279,6 +276,14 @@
         @pl.when(k + 1 < NCH)
         def _():
             relay(k + 1)
+
+        @pl.when(k == 0)
+        def _():
+            arrived(ring.at[0, t_partner], s1r.at[0], partner)
+
+        @pl.when(k == 1)
+        def _():
+            arrived(ring.at[pl.ds(1, NCH - 1), t_partner], s1r.at[1], partner)
 
         r_relay(k)
 
@@ -336,8 +341,9 @@
 
 
 def gather_sum(tab, in_p, in_m, third, out, rows, sem):
-    def copy(r):
-        return pltpu.make_async_copy(rows.at[r], out.at[0, :, :, pl.ds(r * BS, BS), :], sem.at[r])
+    def copy(d):
+        place = out.at[0, :, :, pl.ds(d // NB * BS, BS), pl.ds(d % NB * BS, BS)]
+        return pltpu.make_async_copy(rows.at[d], place, sem.at[0])
 
     def fill(own):
         for r in range(NB):
@@ -348,8 +354,8 @@
                     total = total + third[tab[2 * NCH + d]]
                 for e in range(2):
                     for ri in range(2):
-                        rows[r, e, ri, :, j * BS:(j + 1) * BS] = total[e * BS:(e + 1) * BS, ri * BS:(ri + 1) * BS]
-            copy(r).start()
+                        rows[d, e, ri] = total[e * BS:(e + 1) * BS, ri * BS:(ri + 1) * BS]
+                copy(d).start()
 
     @pl.when(tab[3 * NCH] == 1)
     def _():
@@ -359,8 +365,7 @@
     def _():
         fill(False)
 
-    for r in range(NB):
-        copy(r).wait()
+    pltpu.make_async_copy(rows, rows, sem.at[0]).wait()
 
 
 def on_device(green_lesser, coupling, block_list, offsets, shifts, occupation):
@@ -422,7 +427,7 @@
         out_shape=jax.ShapeDtypeStruct(green_lesser.shape, F32),
         in_specs=[smem, vmem, vmem, vmem],
         out_specs=any_spec,
-        scratch_shapes=[pltpu.VMEM((NB, 2, 2, BS, 512), F32), dma((NB,))],
+        scratch_shapes=[pltpu.VMEM((NCH, 2, 2, BS, BS), F32), dma((1,))],
         compiler_params=pltpu.CompilerParams(vmem_limit_bytes=16 * 1024 * 1024),
         name="gather_sum",
     )(tab, in_p, in_m, third)

time: 70.2 us -> 70 us (level)
  no operation moved by 1% of the time
where the time goes in v5:
time: 70 us; the launch traced here: 69.9 us
  Pallas kernels  69.9 us (100%)
    pallas_call x1, Pallas kernels, on_device(): pl.pallas_call(exchange, out_shape=(pltpu.VMEM(chunk, BF16), pltpu.VMEM(c...  67.9 us
    pallas_call x1, Pallas kernels, on_device(): pl.pallas_call(gather_sum, out_shape=jax.ShapeDtypeStruct(green_lesser.sh...  2.04 us

profile of v5, /device:TPU:1, one launch (start us, length us, event | category | flops | bytes accessed | tf_op | source)
XLA Modules:
  0.0 69.9 jit_solution(1331786104741082313)
XLA Ops:
  0.0 67.9 %exchange.1 = (bf16[16,256,256]{2,1,0:T(8,128)(2,1)S(1)}, bf16[16,256,256]{2,1,0:T(8,128)(2,1)S(1)}, f32[16,256,256]{2,1,0:T(8,128)S(1)}, s32[64]{0:T(128)S(4)}) custom-call(bf16[1,2,2,512,512]{4,3,2,1,0:T(8,128)(2,1)} %g_hbm.1, f32[3,4,2,128,128]{4,3,2,1,0:T(8,128)} %cp_hbm.1, s32[3,2,4]{2,1,0:T(2,128)} %bitcast.1, s32[3]{0:T(128)} %off_hbm.1, s32[3]{0:T(128)} %sh_hbm.1, ...), custom_call_target="tpu_custom_call" | custom-call | tf_op jit(solution)/shard_map/exchange/pallas_call | solution.py:378
  67.9 2.0 %gather_sum.1 = f32[1,2,2,512,512]{4,3,2,1,0:T(8,128)} custom-call(s32[64]{0:T(128)S(4)} %get-tuple-element.9.tab, bf16[16,256,256]{2,1,0:T(8,128)(2,1)S(1)} %get-tuple-element.10.in_p, bf16[16,256,256]{2,1,0:T(8,128)(2,1)S(1)} %get-tuple-element.11.in_m, f32[16,256,256]{2,1,0:T(8,128)S(1)} %get-tuple-element.12.third), custom_call_target="tpu_custom_call" | custom-call | tf_op jit(solution)/shard_map/gather_sum/pallas_call | solution.py:425

commit v6 on v5

--- a/solution.py
+++ b/solution.py
@@ -77,18 +77,20 @@
             ring.at[k, t_own], ring.at[k, 2 * lo + 2 * c], sent.at[0], s1r.at[sem],
             device_id=partner, device_id_type=MESH)
 
-    def c_mate(k):
-        return pltpu.make_async_remote_copy(
-            ring.at[k, t_own], ring.at[k, t_own], sent.at[1], s2r.at[k], device_id=mate, device_id_type=MESH)
+    def c_mate(k, h):
+        return pltpu.make_async_remote_copy(
+            ring.at[k, t_own, h], ring.at[k, t_own, h], sent.at[1], s2r.at[k, h],
+            device_id=mate, device_id_type=MESH)
 
     def c_relay(k):
         return pltpu.make_async_remote_copy(
             ring.at[k, t_swp], ring.at[k, 2 - 2 * lo + 2 * c], sent.at[2], s3r.at[k],
             device_id=partner, device_id_type=MESH)
 
-    def c_y(k):
-        return pltpu.make_async_remote_copy(
-            ring.at[k, 1 + 2 * c], ring.at[k, 4 - 4 * c], sent.at[3], s4r.at[k], device_id=ydev, device_id_type=MESH)
+    def c_y(k, h):
+        return pltpu.make_async_remote_copy(
+            ring.at[k, 1 + 2 * c, h], ring.at[k, 4 - 4 * c, h], sent.at[3], s4r.at[k, h],
+            device_id=ydev, device_id_type=MESH)
 
     def c_up(k):
         return pltpu.make_async_remote_copy(
@@ -102,28 +104,31 @@
         pltpu.make_async_remote_copy(
             target, target, sent.at[0], sem, device_id=device, device_id_type=MESH).wait_recv()
 
-    def r_mate(k):
-        arrived(ring.at[k, t_swp], s2r.at[k], mate)
+    def r_mate(k, h):
+        arrived(ring.at[k, t_swp, h], s2r.at[k, h], mate)
 
     def r_relay(k):
         arrived(ring.at[k, 4 - 2 * lo - 2 * c], s3r.at[k], partner)
 
     def r_y(k):
-        arrived(ring.at[k, 4 * c], s4r.at[k], ydev)
+        for h in range(2):
+            arrived(ring.at[k, 4 * c, h], s4r.at[k, h], ydev)
 
     t_partner = 2 * lo + 2 - 2 * c
     y_own = has_y & (lo == c)
     y_relay = has_y & (lo != c)
 
     def send_mate(k):
-        c_mate(k).start()
+        for h in range(2):
+            c_mate(k, h).start()
 
     def send_chip(k, sem):
         c_partner(k, sem).start()
 
         @pl.when(y_own)
         def _():
-            c_y(k).start()
+            for h in range(2):
+                c_y(k, h).start()
 
     g_copy(0).wait()
     pl.semaphore_wait(barrier, 3 + (z > 0).astype(jnp.int32) + at_top)
@@ -206,11 +211,12 @@
 
 
     def relay(k):
-        r_mate(k)
-
-        @pl.when(y_relay)
-        def _():
-            c_y(k).start()
+        for h in range(2):
+            r_mate(k, h)
+
+            @pl.when(y_relay)
+            def _():
+                c_y(k, h).start()
 
         c_relay(k).start()
 
@@ -411,9 +417,9 @@
             dma((6,)),
             dma((2,)),
             dma((2,)),
+            dma((NCH, 2)),
             dma((NCH,)),
-            dma((NCH,)),
-            dma((NCH,)),
+            dma((NCH, 2)),
         ],
         compiler_params=pltpu.CompilerParams(
             collective_id=0, has_side_effects=True, vmem_limit_bytes=32 * 1024 * 1024),

time: 70 us -> 69.8 us (level)
  no operation moved by 1% of the time
where the time goes in v6:
time: 69.8 us; the launch traced here: 69.6 us
  Pallas kernels  69.6 us (100%)
    pallas_call x1, Pallas kernels, on_device(): pl.pallas_call(exchange, out_shape=(pltpu.VMEM(chunk, BF16), pltpu.VMEM(c...  67.6 us
    pallas_call x1, Pallas kernels, on_device(): pl.pallas_call(gather_sum, out_shape=jax.ShapeDtypeStruct(green_lesser.sh...  2.04 us

profile of v6, /device:TPU:1, one launch (start us, length us, event | category | flops | bytes accessed | tf_op | source)
XLA Modules:
  0.0 69.6 jit_solution(16489253674719040259)
XLA Ops:
  0.0 67.6 %exchange.1 = (bf16[16,256,256]{2,1,0:T(8,128)(2,1)S(1)}, bf16[16,256,256]{2,1,0:T(8,128)(2,1)S(1)}, f32[16,256,256]{2,1,0:T(8,128)S(1)}, s32[64]{0:T(128)S(4)}) custom-call(bf16[1,2,2,512,512]{4,3,2,1,0:T(8,128)(2,1)} %g_hbm.1, f32[3,4,2,128,128]{4,3,2,1,0:T(8,128)} %cp_hbm.1, s32[3,2,4]{2,1,0:T(2,128)} %bitcast.1, s32[3]{0:T(128)} %off_hbm.1, s32[3]{0:T(128)} %sh_hbm.1, ...), custom_call_target="tpu_custom_call" | custom-call | tf_op jit(solution)/shard_map/exchange/pallas_call | solution.py:384
  67.6 2.0 %gather_sum.1 = f32[1,2,2,512,512]{4,3,2,1,0:T(8,128)} custom-call(s32[64]{0:T(128)S(4)} %get-tuple-element.9.tab, bf16[16,256,256]{2,1,0:T(8,128)(2,1)S(1)} %get-tuple-element.10.in_p, bf16[16,256,256]{2,1,0:T(8,128)(2,1)S(1)} %get-tuple-element.11.in_m, f32[16,256,256]{2,1,0:T(8,128)S(1)} %get-tuple-element.12.third), custom_call_target="tpu_custom_call" | custom-call | tf_op jit(solution)/shard_map/gather_sum/pallas_call | solution.py:431
